TPU v7x, 32 devices: a whole 2x2x4 slice. The times are simulated.
32 devices in a mesh: ray: 4 (over x, core), vox: 8 (over z, y).
Axes of the slice: x: 2, y: 2, z: 4, core: 2. Of those that a mesh axis runs over, the one named last changes fastest.
Arguments:
- tiles: float32 [2048, 128, 128], P(('ray', 'vox')), may hold values from -0.25 to 0.25
- tile_ray: int32 [2048], P(('ray', 'vox')), may hold values from 0 to 15
- tile_vox: int32 [2048], P(('ray', 'vox')), may hold values from 0 to 511, as said below
- tile_count: int32 [32], P(('ray', 'vox')), may hold values from 1 to 64, as said below
- travel: float32 [512, 128], P(('ray', 'vox')), may hold values from -6 to 6
Outputs:
- solution: float32 [512, 128], P('vox')
- direction: float32 [512, 128], P('vox')
Inputs may be any that keep to these rules, and one draw needn't show every extreme that they name: `tile_count`: each entry is 1 to 64; some device has exactly 64 live slots. Among the 64 slots of one device (live or not), at most 16 have voxel blocks in the same range of 64 blocks (same tile_vox // 64); on every device some range is named by exactly 16 slots.
All inputs are finite; a program needn't handle non-finite values.
Results may differ from a plain program's by a relative error of at most 0.00017.
Values sent between devices are 32-bit elements; how exact they have to be, the bound alone decides.
No kernel may reach another device: no remote copies, remote signals or barrier semaphores. Data moves between devices by JAX's collectives and lax.ppermute only.
A program may use at most 64 MiB of HBM per device.

v0:
```python
import jax
import jax.numpy as jnp
from jax import lax
from jax.sharding import PartitionSpec as P

VBD = 64
ITERS = 2
HIGH = lax.Precision.HIGHEST


def on_device(tiles, tile_ray, tile_vox, tile_count, travel):
    n_vox = lax.axis_size("vox")
    blocks_all = VBD * n_vox
    tile_num = tiles.shape[0]
    ray_blocks = travel.shape[0]
    width = travel.shape[1]
    live = (jnp.arange(tile_num, dtype=jnp.int32) < tile_count[0]).astype(jnp.float32)[:, None]
    selector = (tile_ray[None, :] == jnp.arange(ray_blocks, dtype=jnp.int32)[:, None]).astype(
        jnp.float32
    )

    def backward(ray_vec):
        rows_in = jnp.dot(selector.T, ray_vec, precision=HIGH)
        prod = jnp.einsum("tij,ti->tj", tiles, rows_in, precision=HIGH) * live
        partial_sum = jnp.zeros((blocks_all, width), jnp.float32).at[tile_vox].add(prod)
        owned = lax.psum_scatter(partial_sum, "vox", scatter_dimension=0, tiled=True)
        return lax.psum(owned, "ray")

    def ray_length(ray_vec):
        return jnp.sqrt(lax.psum(jnp.sum(ray_vec * ray_vec), ("ray", "vox")))

    def vox_length(vox_vec):
        return jnp.sqrt(lax.psum(jnp.sum(vox_vec * vox_vec), "vox"))

    beta_now = ray_length(travel)
    ray_vec = travel / beta_now
    vox_vec = backward(ray_vec)
    alpha_now = vox_length(vox_vec)
    vox_vec = vox_vec / alpha_now
    direction = vox_vec
    solution = jnp.zeros_like(vox_vec)
    phibar = beta_now
    rhobar = alpha_now
    for step in range(ITERS):
        whole = lax.all_gather(vox_vec, "vox", axis=0, tiled=True)
        forward_prod = jnp.einsum("tij,tj->ti", tiles, whole[tile_vox], precision=HIGH) * live
        ray_vec = jnp.dot(selector, forward_prod, precision=HIGH) - alpha_now * ray_vec
        beta_now = ray_length(ray_vec)
        ray_vec = ray_vec / beta_now
        vox_vec = backward(ray_vec) - beta_now * vox_vec
        alpha_now = vox_length(vox_vec)
        vox_vec = vox_vec / alpha_now
        rho_val = jnp.sqrt(rhobar * rhobar + beta_now * beta_now)
        cosine = rhobar / rho_val
        sine_val = beta_now / rho_val
        theta_val = sine_val * alpha_now
        rhobar = -cosine * alpha_now
        phi_val = cosine * phibar
        phibar = sine_val * phibar
        solution = solution + phi_val / rho_val * direction
        direction = vox_vec - theta_val / rho_val * direction
    return (solution, direction)


def solution(mesh):
    return jax.shard_map(
        on_device,
        mesh=mesh,
        in_specs=(
            P(("ray", "vox"), None, None),
            P(("ray", "vox")),
            P(("ray", "vox")),
            P(("ray", "vox")),
            P(("ray", "vox"), None),
        ),
        out_specs=(P("vox", None), P("vox", None)),
        check_vma=False,
    )
```

profile of v0, /device:TPU:0, one launch (start us, length us, event | category | flops | bytes accessed | tf_op | source)
XLA Modules:
  0.0 524.3 jit_solution(6376675607895804721)
XLA Ops:
  7.2 1.3 multiply_reduce_fusion.5
  8.5 42.2 %psum.63 = f32[]{:T(128)} all-reduce(f32[]{:T(128)} %multiply_reduce_fusion.5), channel_id=1, replica_groups=mesh['ray'=4,'vox'=8] {'ray','vox'}, use_global_device_ids=true, to_apply=%region_1.0 | all-reduce | flops 1 | bytes 8 | tf_op jit(solution)/shard_map/psum | solution.py:30
  51.4 0.7 compare_select_fusion
  52.7 0.9 fusion.19
  53.7 5.3 %fusion.26 = f32[64,1,128]{2,1,0:T(1,128)S(1)} fusion(f32[64,128,1]{1,2,0:T(1,128)S(1)} %bitcast.43, f32[64,128,128]{2,1,0:T(8,128)} %param.5), kind=kOutput, calls=%fused_computation.52 | convolution fusion | flops 12582912 | bytes 4259840 | tf_op jit(solution)/shard_map/tij,ti->tj/dot_general | solution.py:24
  59.0 1.5 scatter_custom_fusion
  60.6 61.7 %reduce-scatter.4.cloned.1.call-done = f32[64,128]{1,0:T(8,128)} async-done(((f32[512,128]{1,0:T(8,128)}), f32[64,128]{1,0:T(8,128)}) %reduce-scatter.4.cloned.1.call-update) | async-done | bytes 32784 | tf_op jit(solution)/shard_map/reduce_scatter | solution.py:26
  122.3 10.8 %psum.64 = f32[64,128]{1,0:T(8,128)S(1)} all-reduce(f32[64,128]{1,0:T(8,128)} %reduce-scatter.4.cloned.1.call-done), channel_id=1, replica_groups=mesh['ray'=4,'vox'=8] {'ray'}, use_global_device_ids=true, to_apply=%region_4.0 | all-reduce | flops 8192 | bytes 65536 | tf_op jit(solution)/shard_map/psum | solution.py:27
  133.1 0.6 multiply_reduce_fusion.2
  133.7 20.1 %psum.65 = f32[]{:T(128)} all-reduce(f32[]{:T(128)} %multiply_reduce_fusion.2), channel_id=1, replica_groups=mesh['ray'=4,'vox'=8] {'vox'}, use_global_device_ids=true, to_apply=%region_6.0 | all-reduce | flops 1 | bytes 8 | tf_op jit(solution)/shard_map/psum | solution.py:33
  154.5 30.9 %all_gather.6 = f32[512,128]{1,0:T(8,128)S(1)} all-gather(f32[64,128]{1,0:T(8,128)S(1)} %broadcast_divide_fusion.1), channel_id=1, replica_groups=mesh['ray'=4,'vox'=8] {'vox'}, dimensions={0}, use_global_device_ids=true | all-gather | bytes 294912 | tf_op jit(solution)/shard_map/all_gather | solution.py:45
  185.4 0.6 gather_fusion
  186.0 8.3 %fusion.27 = f32[64,1,128]{2,1,0:T(1,128)S(1)} fusion(f32[64,128,1]{1,2,0:T(1,128)S(1)} %bitcast.40, f32[64,128,128]{2,1,0:T(8,128)} %param.5), kind=kOutput, calls=%fused_computation.53 | convolution fusion | flops 12582912 | bytes 4259840 | tf_op jit(solution)/shard_map/tij,tj->ti/dot_general | solution.py:46
  194.3 0.8 multiply_reduce_fusion.4
  195.2 37.1 %psum.66 = f32[]{:T(128)} all-reduce(f32[]{:T(128)} %get-tuple-element.4), channel_id=1, replica_groups=mesh['ray'=4,'vox'=8] {'ray','vox'}, use_global_device_ids=true, to_apply=%region_8.0 | all-reduce | flops 1 | bytes 8 | tf_op jit(solution)/shard_map/psum | solution.py:30
  233.2 5.3 %fusion.28 = f32[64,1,128]{2,1,0:T(1,128)S(1)} fusion(f32[64,128,1]{1,2,0:T(1,128)S(1)} %bitcast.44, f32[64,128,128]{2,1,0:T(8,128)} %param.5), kind=kOutput, calls=%fused_computation.54 | convolution fusion | flops 12582912 | bytes 4259840 | tf_op jit(solution)/shard_map/tij,ti->tj/dot_general | solution.py:24
  238.5 1.5 scatter_custom_fusion.1
  240.1 63.4 %reduce-scatter.6.cloned.1.call-done = f32[64,128]{1,0:T(8,128)} async-done(((f32[512,128]{1,0:T(8,128)}), f32[64,128]{1,0:T(8,128)}) %reduce-scatter.6.cloned.1.call-update) | async-done | bytes 32784 | tf_op jit(solution)/shard_map/reduce_scatter | solution.py:26
  303.4 10.8 %psum.67 = f32[64,128]{1,0:T(8,128)S(1)} all-reduce(f32[64,128]{1,0:T(8,128)} %reduce-scatter.6.cloned.1.call-done), channel_id=1, replica_groups=mesh['ray'=4,'vox'=8] {'ray'}, use_global_device_ids=true, to_apply=%region_11.0 | all-reduce | flops 8192 | bytes 65536 | tf_op jit(solution)/shard_map/psum | solution.py:27
  314.2 0.6 multiply_reduce_fusion.1
  314.9 20.1 %psum.68 = f32[]{:T(128)} all-reduce(f32[]{:T(128)} %multiply_reduce_fusion.1), channel_id=1, replica_groups=mesh['ray'=4,'vox'=8] {'vox'}, use_global_device_ids=true, to_apply=%region_13.0 | all-reduce | flops 1 | bytes 8 | tf_op jit(solution)/shard_map/psum | solution.py:33
  335.7 31.1 %all_gather.7 = f32[512,128]{1,0:T(8,128)S(1)} all-gather(f32[64,128]{1,0:T(8,128)S(1)} %broadcast_divide_fusion), channel_id=1, replica_groups=mesh['ray'=4,'vox'=8] {'vox'}, dimensions={0}, use_global_device_ids=true | all-gather | bytes 294912 | tf_op jit(solution)/shard_map/all_gather | solution.py:45
  367.3 8.3 %fusion.29 = f32[64,1,128]{2,1,0:T(1,128)S(1)} fusion(f32[64,128,1]{1,2,0:T(1,128)S(1)} %bitcast.38, f32[64,128,128]{2,1,0:T(8,128)} %param.5), kind=kOutput, calls=%fused_computation.55 | convolution fusion | flops 12582912 | bytes 4259840 | tf_op jit(solution)/shard_map/tij,tj->ti/dot_general | solution.py:46
  375.6 0.8 multiply_reduce_fusion.3
  376.4 37.1 %psum.69 = f32[]{:T(128)} all-reduce(f32[]{:T(128)} %get-tuple-element.6), channel_id=1, replica_groups=mesh['ray'=4,'vox'=8] {'ray','vox'}, use_global_device_ids=true, to_apply=%region_15.0 | all-reduce | flops 1 | bytes 8 | tf_op jit(solution)/shard_map/psum | solution.py:30
  414.5 5.3 %fusion.30 = f32[64,1,128]{2,1,0:T(1,128)S(1)} fusion(f32[64,128,1]{1,2,0:T(1,128)S(1)} %bitcast.42, f32[64,128,128]{2,1,0:T(8,128)} %param.5), kind=kOutput, calls=%fused_computation.56 | convolution fusion | flops 12582912 | bytes 4259840 | tf_op jit(solution)/shard_map/tij,ti->tj/dot_general | solution.py:24
  419.8 1.5 scatter_custom_fusion.2
  421.7 63.1 %reduce-scatter.8.cloned.1.call-done = f32[64,128]{1,0:T(8,128)} async-done(((f32[512,128]{1,0:T(8,128)}), f32[64,128]{1,0:T(8,128)}) %reduce-scatter.8.cloned.1.call-update) | async-done | bytes 32784 | tf_op jit(solution)/shard_map/reduce_scatter | solution.py:26
  484.8 10.8 %psum.70 = f32[64,128]{1,0:T(8,128)S(1)} all-reduce(f32[64,128]{1,0:T(8,128)} %reduce-scatter.8.cloned.1.call-done), channel_id=1, replica_groups=mesh['ray'=4,'vox'=8] {'ray'}, use_global_device_ids=true, to_apply=%region_18.0 | all-reduce | flops 8192 | bytes 65536 | tf_op jit(solution)/shard_map/psum | solution.py:27
  495.6 0.6 multiply_reduce_fusion
  496.2 20.1 %psum.71 = f32[]{:T(128)} all-reduce(f32[]{:T(128)} %multiply_reduce_fusion), channel_id=1, replica_groups=mesh['ray'=4,'vox'=8] {'vox'}, use_global_device_ids=true, to_apply=%region_20.0 | all-reduce | flops 1 | bytes 8 | tf_op jit(solution)/shard_map/psum | solution.py:33
  517.1 0.7 multiply_subtract_fusion
  (17 shorter events, 1.2 us)
Async XLA Ops:
  7.2 115.2 %reduce-scatter.4.cloned.1.call-start = ((), (), s32[]{:S(2)}) async-start(), calls=%async_computation.3 | async-start | bytes 294912 | tf_op jit(solution)/shard_map/reduce_scatter | solution.py:26
  53.7 140.7 %copy-start = (f32[16,128]{1,0:T(8,128)S(1)}, f32[16,128]{1,0:T(8,128)}, u32[]{:S(2)}) copy-start(f32[16,128]{1,0:T(8,128)} %param.9) | copy-start | bytes 24580
  53.7 140.7 %copy-start.1 = (s32[64]{0:T(128)S(1)}, s32[64]{0:T(128)}, u32[]{:S(2)}) copy-start(s32[64]{0:T(128)} %param.6) | copy-start | bytes 772
  60.5 242.9 %reduce-scatter.6.cloned.1.call-start = ((), (), s32[]{:S(2)}) async-start(), calls=%async_computation.4 | async-start | bytes 294912 | tf_op jit(solution)/shard_map/reduce_scatter | solution.py:26
  240.0 244.7 %reduce-scatter.8.cloned.1.call-start = ((), (), s32[]{:S(2)}) async-start(), calls=%async_computation.5 | async-start | bytes 294912 | tf_op jit(solution)/shard_map/reduce_scatter | solution.py:26
Sparse Core Ops, SparseCore 0:
  60.7 61.6 reduce-scatter.3
  240.2 63.2 reduce-scatter.5
  421.5 63.2 reduce-scatter.7
where the time goes:
time: 526 us; the launch traced here: 524 us
  blocking collectives  271 us (52%)
  waiting for transfers between devices  188 us (36%)
  matrix products  35.5 us (7%)
  between operations  19.1 us (4%)
  other arithmetic  9.11 us (2%)
    reduce_scatter x3, waiting for transfers between devices, backward(): lax.psum_scatter(partial_sum, 'vox', scatter_dimension=0, tiled=True)  188 us
    psum x3, blocking collectives, ray_length(): return jnp.sqrt(lax.psum(jnp.sum(ray_vec * ray_vec), ('ray', 'vox')))  116 us
    all_gather x2, blocking collectives, on_device(): whole = lax.all_gather(vox_vec, 'vox', axis=0, tiled=True)  62 us
    psum x3, blocking collectives, vox_length(): return jnp.sqrt(lax.psum(jnp.sum(vox_vec * vox_vec), 'vox'))  60.2 us
    psum x3, blocking collectives, backward(): return lax.psum(owned, 'ray')  32.4 us
    dot_general x2, matrix products, on_device(): jnp.einsum('tij,tj->ti', tiles, whole[tile_vox], precision=HIGH) * live  16.6 us
    dot_general x3, matrix products, backward(): prod = jnp.einsum('tij,ti->tj', tiles, rows_in, precision=HIGH) * live  15.8 us
  transfers between devices with their start and end apart: 3, of which 3 were waited for; matrix products, arithmetic and copies ran while one was open for 0% of the time, Pallas kernels for 0%

commit v1 on v0

--- a/solution.py
+++ b/solution.py
@@ -42,7 +42,15 @@
     phibar = beta_now
     rhobar = alpha_now
     for step in range(ITERS):
-        whole = lax.all_gather(vox_vec, "vox", axis=0, tiled=True)
+        nodes = lax.axis_size("vox")
+        tray = tuple(((q, (q + 1) % nodes) for q in range(nodes)))
+        w1 = [None] * nodes
+        w1[nodes - 1] = vox_vec
+        for k in range(nodes - 2, -1, -1):
+            w1[k] = lax.ppermute(w1[k + 1], perm=tray, axis_name="vox")
+        base_arr = jnp.concatenate(w1, axis=0)
+        outer = (lax.axis_index("vox") + 1) * vox_vec.shape[0]
+        whole = jnp.roll(base_arr, outer, axis=0)
         forward_prod = jnp.einsum("tij,tj->ti", tiles, whole[tile_vox], precision=HIGH) * live
         ray_vec = jnp.dot(selector, forward_prod, precision=HIGH) - alpha_now * ray_vec
         beta_now = ray_length(ray_vec)

time: 526 us -> 557 us (1.059)
  waiting for transfers between devices: 188 us -> 281 us
  blocking collectives: 271 us -> 209 us
    ppermute x0 -> x14, waiting for transfers between devices: none -> 92.6 us  [on_device(): w1[k] = lax.ppermute(w1[k + 1], perm=tray, axis_name='vox')]
    all_gather x2 -> x0, blocking collectives: 62 us -> none  [on_device(): whole = lax.all_gather(vox_vec, 'vox', axis=0, tiled=True)]
  transfers between devices with their start and end apart: 3 -> 17, of which waited for: 3 -> 17; matrix products, arithmetic and copies ran while one was open for 0% -> 0% of each run, Pallas kernels for 0% -> 0%
where the time goes in v1:
time: 557 us; the launch traced here: 556 us
  waiting for transfers between devices  281 us (50%)
  blocking collectives  209 us (38%)
  matrix products  35.5 us (6%)
  between operations  19.2 us (3%)
  other arithmetic  9.45 us (2%)
    reduce_scatter x3, waiting for transfers between devices, backward(): lax.psum_scatter(partial_sum, 'vox', scatter_dimension=0, tiled=True)  189 us
    psum x3, blocking collectives, ray_length(): return jnp.sqrt(lax.psum(jnp.sum(ray_vec * ray_vec), ('ray', 'vox')))  116 us
    ppermute x14, waiting for transfers between devices, on_device(): w1[k] = lax.ppermute(w1[k + 1], perm=tray, axis_name='vox')  92.6 us
    psum x3, blocking collectives, vox_length(): return jnp.sqrt(lax.psum(jnp.sum(vox_vec * vox_vec), 'vox'))  60.2 us
    psum x3, blocking collectives, backward(): return lax.psum(owned, 'ray')  32.4 us
    dot_general x2, matrix products, on_device(): jnp.einsum('tij,tj->ti', tiles, whole[tile_vox], precision=HIGH) * live  16.6 us
    dot_general x3, matrix products, backward(): prod = jnp.einsum('tij,ti->tj', tiles, rows_in, precision=HIGH) * live  15.8 us
  transfers between devices with their start and end apart: 17, of which 17 were waited for; matrix products, arithmetic and copies ran while one was open for 0% of the time, Pallas kernels for 0%

profile of v1, /device:TPU:0, one launch (start us, length us, event | category | flops | bytes accessed | tf_op | source)
XLA Modules:
  0.0 555.9 jit_solution(8006494841622293227)
XLA Ops:
  8.5 42.2 %psum.63 = f32[]{:T(128)} all-reduce(f32[]{:T(128)} %multiply_reduce_fusion.5), channel_id=1, replica_groups=mesh['ray'=4,'vox'=8] {'ray','vox'}, use_global_device_ids=true, to_apply=%region_1.0 | all-reduce | flops 1 | bytes 8 | tf_op jit(solution)/shard_map/psum | solution.py:30
  53.7 5.3 fusion.28
  58.9 1.5 scatter_custom_fusion
  60.6 61.7 %reduce-scatter.4.cloned.1.call-done = f32[64,128]{1,0:T(8,128)} async-done(((f32[512,128]{1,0:T(8,128)}), f32[64,128]{1,0:T(8,128)}) %reduce-scatter.4.cloned.1.call-update) | async-done | bytes 32784 | tf_op jit(solution)/shard_map/reduce_scatter | solution.py:26
  122.3 10.8 %psum.64 = f32[64,128]{1,0:T(8,128)S(1)} all-reduce(f32[64,128]{1,0:T(8,128)} %reduce-scatter.4.cloned.1.call-done), channel_id=1, replica_groups=mesh['ray'=4,'vox'=8] {'ray'}, use_global_device_ids=true, to_apply=%region_4.0 | all-reduce | flops 8192 | bytes 65536 | tf_op jit(solution)/shard_map/psum | solution.py:27
  133.7 20.1 %psum.65 = f32[]{:T(128)} all-reduce(f32[]{:T(128)} %multiply_reduce_fusion.2), channel_id=1, replica_groups=mesh['ray'=4,'vox'=8] {'vox'}, use_global_device_ids=true, to_apply=%region_6.0 | all-reduce | flops 1 | bytes 8 | tf_op jit(solution)/shard_map/psum | solution.py:33
  154.5 6.6 %collective-permute-done = f32[64,128]{1,0:T(8,128)S(1)} collective-permute-done((f32[64,128]{1,0:T(8,128)S(1)}, f32[64,128]{1,0:T(8,128)S(1)}, u32[]{:S(2)}, u32[]{:S(2)}) %collective-permute-start) | collective-permute-done | bytes 32800 | tf_op jit(solution)/shard_map/ppermute | solution.py:50
  161.1 6.7 %collective-permute-done.1 = f32[64,128]{1,0:T(8,128)S(1)} collective-permute-done((f32[64,128]{1,0:T(8,128)S(1)}, f32[64,128]{1,0:T(8,128)S(1)}, u32[]{:S(2)}, u32[]{:S(2)}) %collective-permute-start.1) | collective-permute-done | bytes 32800 | tf_op jit(solution)/shard_map/ppermute | solution.py:50
  167.8 6.6 %collective-permute-done.2 = f32[64,128]{1,0:T(8,128)S(1)} collective-permute-done((f32[64,128]{1,0:T(8,128)S(1)}, f32[64,128]{1,0:T(8,128)S(1)}, u32[]{:S(2)}, u32[]{:S(2)}) %collective-permute-start.2) | collective-permute-done | bytes 32800 | tf_op jit(solution)/shard_map/ppermute | solution.py:50
  174.4 6.6 %collective-permute-done.3 = f32[64,128]{1,0:T(8,128)S(1)} collective-permute-done((f32[64,128]{1,0:T(8,128)S(1)}, f32[64,128]{1,0:T(8,128)S(1)}, u32[]{:S(2)}, u32[]{:S(2)}) %collective-permute-start.3) | collective-permute-done | bytes 32800 | tf_op jit(solution)/shard_map/ppermute | solution.py:50
  181.1 6.6 %collective-permute-done.4 = f32[64,128]{1,0:T(8,128)S(1)} collective-permute-done((f32[64,128]{1,0:T(8,128)S(1)}, f32[64,128]{1,0:T(8,128)S(1)}, u32[]{:S(2)}, u32[]{:S(2)}) %collective-permute-start.4) | collective-permute-done | bytes 32800 | tf_op jit(solution)/shard_map/ppermute | solution.py:50
  187.7 6.6 %collective-permute-done.5 = f32[64,128]{1,0:T(8,128)S(1)} collective-permute-done((f32[64,128]{1,0:T(8,128)S(1)}, f32[64,128]{1,0:T(8,128)S(1)}, u32[]{:S(2)}, u32[]{:S(2)}) %collective-permute-start.5) | collective-permute-done | bytes 32800 | tf_op jit(solution)/shard_map/ppermute | solution.py:50
  194.3 6.6 %collective-permute-done.6 = f32[64,128]{1,0:T(8,128)S(1)} collective-permute-done((f32[64,128]{1,0:T(8,128)S(1)}, f32[64,128]{1,0:T(8,128)S(1)}, u32[]{:S(2)}, u32[]{:S(2)}) %collective-permute-start.6) | collective-permute-done | bytes 32800 | tf_op jit(solution)/shard_map/ppermute | solution.py:50
  201.8 8.3 %fusion.29 = f32[64,1,128]{2,1,0:T(1,128)S(1)} fusion(f32[64,128,1]{1,2,0:T(1,128)S(1)} %bitcast.40, f32[64,128,128]{2,1,0:T(8,128)} %param.7), kind=kOutput, calls=%fused_computation.75 | convolution fusion | flops 12582912 | bytes 4259840 | tf_op jit(solution)/shard_map/tij,tj->ti/dot_general | solution.py:54
  210.9 37.1 %psum.66 = f32[]{:T(128)} all-reduce(f32[]{:T(128)} %get-tuple-element.5), channel_id=1, replica_groups=mesh['ray'=4,'vox'=8] {'ray','vox'}, use_global_device_ids=true, to_apply=%region_8.10 | all-reduce | flops 1 | bytes 8 | tf_op jit(solution)/shard_map/psum | solution.py:30
  248.9 5.3 fusion.30
  255.8 63.6 %reduce-scatter.6.cloned.1.call-done = f32[64,128]{1,0:T(8,128)} async-done(((f32[512,128]{1,0:T(8,128)}), f32[64,128]{1,0:T(8,128)}) %reduce-scatter.6.cloned.1.call-update) | async-done | bytes 32784 | tf_op jit(solution)/shard_map/reduce_scatter | solution.py:26
  319.4 10.8 %psum.67 = f32[64,128]{1,0:T(8,128)S(1)} all-reduce(f32[64,128]{1,0:T(8,128)} %reduce-scatter.6.cloned.1.call-done), channel_id=1, replica_groups=mesh['ray'=4,'vox'=8] {'ray'}, use_global_device_ids=true, to_apply=%region_11.13 | all-reduce | flops 8192 | bytes 65536 | tf_op jit(solution)/shard_map/psum | solution.py:27
  330.8 20.0 %psum.68 = f32[]{:T(128)} all-reduce(f32[]{:T(128)} %multiply_reduce_fusion.1), channel_id=1, replica_groups=mesh['ray'=4,'vox'=8] {'vox'}, use_global_device_ids=true, to_apply=%region_13.15 | all-reduce | flops 1 | bytes 8 | tf_op jit(solution)/shard_map/psum | solution.py:33
  351.6 6.6 %collective-permute-done.7 = f32[64,128]{1,0:T(8,128)S(1)} collective-permute-done((f32[64,128]{1,0:T(8,128)S(1)}, f32[64,128]{1,0:T(8,128)S(1)}, u32[]{:S(2)}, u32[]{:S(2)}) %collective-permute-start.7) | collective-permute-done | bytes 32800 | tf_op jit(solution)/shard_map/ppermute | solution.py:50
  358.2 6.7 %collective-permute-done.8 = f32[64,128]{1,0:T(8,128)S(1)} collective-permute-done((f32[64,128]{1,0:T(8,128)S(1)}, f32[64,128]{1,0:T(8,128)S(1)}, u32[]{:S(2)}, u32[]{:S(2)}) %collective-permute-start.8) | collective-permute-done | bytes 32800 | tf_op jit(solution)/shard_map/ppermute | solution.py:50
  364.9 6.6 %collective-permute-done.9 = f32[64,128]{1,0:T(8,128)S(1)} collective-permute-done((f32[64,128]{1,0:T(8,128)S(1)}, f32[64,128]{1,0:T(8,128)S(1)}, u32[]{:S(2)}, u32[]{:S(2)}) %collective-permute-start.9) | collective-permute-done | bytes 32800 | tf_op jit(solution)/shard_map/ppermute | solution.py:50
  371.5 6.6 %collective-permute-done.10 = f32[64,128]{1,0:T(8,128)S(1)} collective-permute-done((f32[64,128]{1,0:T(8,128)S(1)}, f32[64,128]{1,0:T(8,128)S(1)}, u32[]{:S(2)}, u32[]{:S(2)}) %collective-permute-start.10) | collective-permute-done | bytes 32800 | tf_op jit(solution)/shard_map/ppermute | solution.py:50
  378.1 6.6 %collective-permute-done.11 = f32[64,128]{1,0:T(8,128)S(1)} collective-permute-done((f32[64,128]{1,0:T(8,128)S(1)}, f32[64,128]{1,0:T(8,128)S(1)}, u32[]{:S(2)}, u32[]{:S(2)}) %collective-permute-start.11) | collective-permute-done | bytes 32800 | tf_op jit(solution)/shard_map/ppermute | solution.py:50
  384.7 6.6 %collective-permute-done.12 = f32[64,128]{1,0:T(8,128)S(1)} collective-permute-done((f32[64,128]{1,0:T(8,128)S(1)}, f32[64,128]{1,0:T(8,128)S(1)}, u32[]{:S(2)}, u32[]{:S(2)}) %collective-permute-start.12) | collective-permute-done | bytes 32800 | tf_op jit(solution)/shard_map/ppermute | solution.py:50
  391.3 6.6 %collective-permute-done.13 = f32[64,128]{1,0:T(8,128)S(1)} collective-permute-done((f32[64,128]{1,0:T(8,128)S(1)}, f32[64,128]{1,0:T(8,128)S(1)}, u32[]{:S(2)}, u32[]{:S(2)}) %collective-permute-start.13) | collective-permute-done | bytes 32800 | tf_op jit(solution)/shard_map/ppermute | solution.py:50
  398.8 8.3 %fusion.31 = f32[64,1,128]{2,1,0:T(1,128)S(1)} fusion(f32[64,128,1]{1,2,0:T(1,128)S(1)} %bitcast.38, f32[64,128,128]{2,1,0:T(8,128)} %param.7), kind=kOutput, calls=%fused_computation.77 | convolution fusion | flops 12582912 | bytes 4259840 | tf_op jit(solution)/shard_map/tij,tj->ti/dot_general | solution.py:54
  407.9 37.1 %psum.69 = f32[]{:T(128)} all-reduce(f32[]{:T(128)} %get-tuple-element.7), channel_id=1, replica_groups=mesh['ray'=4,'vox'=8] {'ray','vox'}, use_global_device_ids=true, to_apply=%region_15.17 | all-reduce | flops 1 | bytes 8 | tf_op jit(solution)/shard_map/psum | solution.py:30
  445.9 5.3 fusion.32
  453.1 63.2 %reduce-scatter.8.cloned.1.call-done = f32[64,128]{1,0:T(8,128)} async-done(((f32[512,128]{1,0:T(8,128)}), f32[64,128]{1,0:T(8,128)}) %reduce-scatter.8.cloned.1.call-update) | async-done | bytes 32784 | tf_op jit(solution)/shard_map/reduce_scatter | solution.py:26
  516.4 10.8 %psum.70 = f32[64,128]{1,0:T(8,128)S(1)} all-reduce(f32[64,128]{1,0:T(8,128)} %reduce-scatter.8.cloned.1.call-done), channel_id=1, replica_groups=mesh['ray'=4,'vox'=8] {'ray'}, use_global_device_ids=true, to_apply=%region_18.20 | all-reduce | flops 8192 | bytes 65536 | tf_op jit(solution)/shard_map/psum | solution.py:27
  527.8 20.1 %psum.71 = f32[]{:T(128)} all-reduce(f32[]{:T(128)} %multiply_reduce_fusion), channel_id=1, replica_groups=mesh['ray'=4,'vox'=8] {'vox'}, use_global_device_ids=true, to_apply=%region_20.22 | all-reduce | flops 1 | bytes 8 | tf_op jit(solution)/shard_map/psum | solution.py:33
  (61 shorter events, 12.5 us)
Async XLA Ops:
  7.2 115.1 %reduce-scatter.4.cloned.1.call-start = ((), (), s32[]{:S(2)}) async-start(), calls=%async_computation.3 | async-start | bytes 294912 | tf_op jit(solution)/shard_map/reduce_scatter | solution.py:26
  58.9 151.1 %copy-start = (f32[16,128]{1,0:T(8,128)S(1)}, f32[16,128]{1,0:T(8,128)}, u32[]{:S(2)}) copy-start(f32[16,128]{1,0:T(8,128)} %param.11) | copy-start | bytes 24580
  58.9 151.1 %copy-start.1 = (s32[64]{0:T(128)S(1)}, s32[64]{0:T(128)}, u32[]{:S(2)}) copy-start(s32[64]{0:T(128)} %param.8) | copy-start | bytes 772
  60.5 258.8 %reduce-scatter.6.cloned.1.call-start = ((), (), s32[]{:S(2)}) async-start(), calls=%async_computation.4 | async-start | bytes 294912 | tf_op jit(solution)/shard_map/reduce_scatter | solution.py:26
  154.5 6.7 %collective-permute-start = (f32[64,128]{1,0:T(8,128)S(1)}, f32[64,128]{1,0:T(8,128)S(1)}, u32[]{:S(2)}, u32[]{:S(2)}) collective-permute-start(f32[64,128]{1,0:T(8,128)S(1)} %broadcast_divide_fusion.1), channel_id=1, source_target_pairs={{0,1},{1,2},{2,3},{3,4},{4,5},{5,6},{6,7},{7,0},{8,9},{9,10},{10,1... | collective-permute-start | bytes 98312 | tf_op jit(solution)/shard_map/ppermute | solution.py:50
  161.1 6.7 %collective-permute-start.1 = (f32[64,128]{1,0:T(8,128)S(1)}, f32[64,128]{1,0:T(8,128)S(1)}, u32[]{:S(2)}, u32[]{:S(2)}) collective-permute-start(f32[64,128]{1,0:T(8,128)S(1)} %collective-permute-done), channel_id=1, source_target_pairs={{0,1},{1,2},{2,3},{3,4},{4,5},{5,6},{6,7},{7,0},{8,9},{9,10},{10,1... | collective-permute-start | bytes 98312 | tf_op jit(solution)/shard_map/ppermute | solution.py:50
  167.8 6.6 %collective-permute-start.2 = (f32[64,128]{1,0:T(8,128)S(1)}, f32[64,128]{1,0:T(8,128)S(1)}, u32[]{:S(2)}, u32[]{:S(2)}) collective-permute-start(f32[64,128]{1,0:T(8,128)S(1)} %collective-permute-done.1), channel_id=1, source_target_pairs={{0,1},{1,2},{2,3},{3,4},{4,5},{5,6},{6,7},{7,0},{8,9},{9,10},{10,1... | collective-permute-start | bytes 98312 | tf_op jit(solution)/shard_map/ppermute | solution.py:50
  174.4 6.6 %collective-permute-start.3 = (f32[64,128]{1,0:T(8,128)S(1)}, f32[64,128]{1,0:T(8,128)S(1)}, u32[]{:S(2)}, u32[]{:S(2)}) collective-permute-start(f32[64,128]{1,0:T(8,128)S(1)} %collective-permute-done.2), channel_id=1, source_target_pairs={{0,1},{1,2},{2,3},{3,4},{4,5},{5,6},{6,7},{7,0},{8,9},{9,10},{10,1... | collective-permute-start | bytes 98312 | tf_op jit(solution)/shard_map/ppermute | solution.py:50
  181.1 6.6 %collective-permute-start.4 = (f32[64,128]{1,0:T(8,128)S(1)}, f32[64,128]{1,0:T(8,128)S(1)}, u32[]{:S(2)}, u32[]{:S(2)}) collective-permute-start(f32[64,128]{1,0:T(8,128)S(1)} %collective-permute-done.3), channel_id=1, source_target_pairs={{0,1},{1,2},{2,3},{3,4},{4,5},{5,6},{6,7},{7,0},{8,9},{9,10},{10,1... | collective-permute-start | bytes 98312 | tf_op jit(solution)/shard_map/ppermute | solution.py:50
  187.7 6.6 %collective-permute-start.5 = (f32[64,128]{1,0:T(8,128)S(1)}, f32[64,128]{1,0:T(8,128)S(1)}, u32[]{:S(2)}, u32[]{:S(2)}) collective-permute-start(f32[64,128]{1,0:T(8,128)S(1)} %collective-permute-done.4), channel_id=1, source_target_pairs={{0,1},{1,2},{2,3},{3,4},{4,5},{5,6},{6,7},{7,0},{8,9},{9,10},{10,1... | collective-permute-start | bytes 98312 | tf_op jit(solution)/shard_map/ppermute | solution.py:50
  194.3 6.6 %collective-permute-start.6 = (f32[64,128]{1,0:T(8,128)S(1)}, f32[64,128]{1,0:T(8,128)S(1)}, u32[]{:S(2)}, u32[]{:S(2)}) collective-permute-start(f32[64,128]{1,0:T(8,128)S(1)} %collective-permute-done.5), channel_id=1, source_target_pairs={{0,1},{1,2},{2,3},{3,4},{4,5},{5,6},{6,7},{7,0},{8,9},{9,10},{10,1... | collective-permute-start | bytes 98312 | tf_op jit(solution)/shard_map/ppermute | solution.py:50
  255.8 260.6 %reduce-scatter.8.cloned.1.call-start = ((), (), s32[]{:S(2)}) async-start(), calls=%async_computation.5 | async-start | bytes 294912 | tf_op jit(solution)/shard_map/reduce_scatter | solution.py:26
  351.5 6.7 %collective-permute-start.7 = (f32[64,128]{1,0:T(8,128)S(1)}, f32[64,128]{1,0:T(8,128)S(1)}, u32[]{:S(2)}, u32[]{:S(2)}) collective-permute-start(f32[64,128]{1,0:T(8,128)S(1)} %broadcast_divide_fusion), channel_id=1, source_target_pairs={{0,1},{1,2},{2,3},{3,4},{4,5},{5,6},{6,7},{7,0},{8,9},{9,10},{10,1... | collective-permute-start | bytes 98312 | tf_op jit(solution)/shard_map/ppermute | solution.py:50
  358.2 6.7 %collective-permute-start.8 = (f32[64,128]{1,0:T(8,128)S(1)}, f32[64,128]{1,0:T(8,128)S(1)}, u32[]{:S(2)}, u32[]{:S(2)}) collective-permute-start(f32[64,128]{1,0:T(8,128)S(1)} %collective-permute-done.7), channel_id=1, source_target_pairs={{0,1},{1,2},{2,3},{3,4},{4,5},{5,6},{6,7},{7,0},{8,9},{9,10},{10,1... | collective-permute-start | bytes 98312 | tf_op jit(solution)/shard_map/ppermute | solution.py:50
  364.9 6.6 %collective-permute-start.9 = (f32[64,128]{1,0:T(8,128)S(1)}, f32[64,128]{1,0:T(8,128)S(1)}, u32[]{:S(2)}, u32[]{:S(2)}) collective-permute-start(f32[64,128]{1,0:T(8,128)S(1)} %collective-permute-done.8), channel_id=1, source_target_pairs={{0,1},{1,2},{2,3},{3,4},{4,5},{5,6},{6,7},{7,0},{8,9},{9,10},{10,1... | collective-permute-start | bytes 98312 | tf_op jit(solution)/shard_map/ppermute | solution.py:50
  371.5 6.6 %collective-permute-start.10 = (f32[64,128]{1,0:T(8,128)S(1)}, f32[64,128]{1,0:T(8,128)S(1)}, u32[]{:S(2)}, u32[]{:S(2)}) collective-permute-start(f32[64,128]{1,0:T(8,128)S(1)} %collective-permute-done.9), channel_id=1, source_target_pairs={{0,1},{1,2},{2,3},{3,4},{4,5},{5,6},{6,7},{7,0},{8,9},{9,10},{10,1... | collective-permute-start | bytes 98312 | tf_op jit(solution)/shard_map/ppermute | solution.py:50
  378.1 6.6 %collective-permute-start.11 = (f32[64,128]{1,0:T(8,128)S(1)}, f32[64,128]{1,0:T(8,128)S(1)}, u32[]{:S(2)}, u32[]{:S(2)}) collective-permute-start(f32[64,128]{1,0:T(8,128)S(1)} %collective-permute-done.10), channel_id=1, source_target_pairs={{0,1},{1,2},{2,3},{3,4},{4,5},{5,6},{6,7},{7,0},{8,9},{9,10},{10,1... | collective-permute-start | bytes 98312 | tf_op jit(solution)/shard_map/ppermute | solution.py:50
  384.7 6.6 %collective-permute-start.12 = (f32[64,128]{1,0:T(8,128)S(1)}, f32[64,128]{1,0:T(8,128)S(1)}, u32[]{:S(2)}, u32[]{:S(2)}) collective-permute-start(f32[64,128]{1,0:T(8,128)S(1)} %collective-permute-done.11), channel_id=1, source_target_pairs={{0,1},{1,2},{2,3},{3,4},{4,5},{5,6},{6,7},{7,0},{8,9},{9,10},{10,1... | collective-permute-start | bytes 98312 | tf_op jit(solution)/shard_map/ppermute | solution.py:50
  391.3 6.6 %collective-permute-start.13 = (f32[64,128]{1,0:T(8,128)S(1)}, f32[64,128]{1,0:T(8,128)S(1)}, u32[]{:S(2)}, u32[]{:S(2)}) collective-permute-start(f32[64,128]{1,0:T(8,128)S(1)} %collective-permute-done.12), channel_id=1, source_target_pairs={{0,1},{1,2},{2,3},{3,4},{4,5},{5,6},{6,7},{7,0},{8,9},{9,10},{10,1... | collective-permute-start | bytes 98312 | tf_op jit(solution)/shard_map/ppermute | solution.py:50
Sparse Core Ops, SparseCore 0:
  60.6 61.6 reduce-scatter.3
  255.9 63.4 reduce-scatter.5
  452.9 63.4 reduce-scatter.7
